TPU v7x, 512 devices: a whole 4x8x8 slice. The times are simulated.
512 devices in a mesh: expert: 64 (over z, y), tp: 8 (over x, core).
Axes of the slice: x: 4, y: 8, z: 8, core: 2. Of those that a mesh axis runs over, the one named last changes fastest.
Arguments:
- cotangent: bfloat16 [8192, 2048], P('expert'), may hold values from -6 to 6
- gates: float32 [8192, 8], P('expert'), may hold values from 0.05 to 0.6
- expert_ids: int32 [8192, 8], P('expert'), may hold values from 0 to 127, all different within a row; in each aligned block of 128 rows (0 to 127, 128 to 255, ...) at most 12 rows name the same one
- saved_gate: bfloat16 [128, 768, 768], P('expert', 'tp'), may hold values from -6 to 6
- saved_up: bfloat16 [128, 768, 768], P('expert', 'tp'), may hold values from -6 to 6
- w_gate: bfloat16 [128, 768, 2048], P('expert', 'tp'), may hold values from -0.125 to 0.125
- w_up: bfloat16 [128, 768, 2048], P('expert', 'tp'), may hold values from -0.125 to 0.125
- w_down: bfloat16 [128, 768, 2048], P('expert', 'tp'), may hold values from -0.21875 to 0.21875
Outputs:
- token_grad: float32 [8192, 2048], P(('expert', 'tp'))
Inputs may be any that keep to these rules, and one draw needn't show every extreme that they name: `expert_ids`: within the 128 tokens of one group, no expert is named by more than 12 route rows, a bound that some block reaches; a token names 8 different experts.
All inputs are finite; a program needn't handle non-finite values.
Results may differ from a plain program's by a relative error of at most 0.0049.
Values may be sent and summed in bfloat16 or wider, within the bound.
A program may use at most 64 MiB of HBM per device.

v0:
```python
import jax
import jax.numpy as jnp
from jax import lax
from jax.sharding import PartitionSpec as P


def route_slots(expert_ids, expert_total):
    flat_ids = expert_ids.reshape(-1)
    one_hot = (flat_ids[:, None] == jnp.arange(expert_total, dtype=jnp.int32)[None, :]).astype(
        jnp.int32
    )
    before = jnp.cumsum(one_hot, axis=0) - one_hot
    return (flat_ids, jnp.sum(before * one_hot, axis=1))


def body(cotangent, gates, expert_ids, saved_gate, saved_up, w_gate, w_up, w_down):
    owners = lax.axis_size("expert")
    row_count, feature_dim = cotangent.shape
    top_count = expert_ids.shape[1]
    local_count, shard_width, slot_count = saved_gate.shape
    capacity = slot_count // owners
    flat_ids, slot_pos = route_slots(expert_ids, local_count * owners)
    target = flat_ids % local_count * slot_count + flat_ids // local_count * capacity + slot_pos
    scaled = (gates[:, :, None] * cotangent.astype(jnp.float32)[:, None, :]).astype(jnp.bfloat16)
    scaled = scaled.reshape(row_count * top_count, feature_dim)
    outgoing = (
        jnp.zeros((local_count * slot_count, feature_dim), jnp.bfloat16).at[target].set(scaled)
    )
    outgoing = outgoing.reshape(local_count, slot_count, feature_dim)
    arrived = lax.all_to_all(outgoing, "expert", split_axis=1, concat_axis=1, tiled=True)
    hidden_grad = jnp.einsum("efd,esd->efs", w_down, arrived, preferred_element_type=jnp.float32)
    gate_value = saved_gate.astype(jnp.float32)
    up_value = saved_up.astype(jnp.float32)
    sigmoid_gate = jax.nn.sigmoid(gate_value)
    up_grad = (hidden_grad * gate_value * sigmoid_gate).astype(jnp.bfloat16)
    gate_grad = (
        hidden_grad * up_value * sigmoid_gate * (1.0 + gate_value * (1.0 - sigmoid_gate))
    ).astype(jnp.bfloat16)
    partial_value = jnp.einsum(
        "efs,efd->esd", gate_grad, w_gate, preferred_element_type=jnp.float32
    )
    partial_value = partial_value + jnp.einsum(
        "efs,efd->esd", up_grad, w_up, preferred_element_type=jnp.float32
    )
    partial_value = partial_value.astype(jnp.bfloat16)
    returned = lax.all_to_all(partial_value, "expert", split_axis=1, concat_axis=1, tiled=True)
    picked = returned.reshape(local_count * slot_count, feature_dim)[target].astype(jnp.float32)
    combined = jnp.sum(picked.reshape(row_count, top_count, feature_dim), axis=1)
    return lax.psum_scatter(combined, "tp", scatter_dimension=0, tiled=True)


def solution(mesh):
    in_specs = (
        P("expert", None),
        P("expert", None),
        P("expert", None),
        P("expert", "tp", None),
        P("expert", "tp", None),
        P("expert", "tp", None),
        P("expert", "tp", None),
        P("expert", "tp", None),
    )
    out_specs = P(("expert", "tp"), None)
    return jax.shard_map(body, mesh=mesh, in_specs=in_specs, out_specs=out_specs, check_vma=False)
```

profile of v0, /device:TPU:1, one launch (start us, length us, event | category | flops | bytes accessed | tf_op | source)
XLA Modules:
  0.0 512.4 jit_solution(17856409927012851818)
XLA Ops:
  6.5 0.0 copy-start
  6.5 0.9 copy.24
  7.4 0.1 eq.31
  7.5 0.1 eq.27
  7.6 0.1 reshape.156
  7.7 0.1 copy.27
  7.8 0.8 copy.29
  8.6 0.1 mul.70
  8.7 0.2 fusion.21
  9.0 0.1 copy.28
  9.1 1.1 convert_element_type.38
  10.2 0.4 fusion.20
  10.6 10.6 %scatter_custom_fusion = bf16[1536,2048]{1,0:T(8,128)(2,1)} fusion(s32[1024]{0:T(1024)S(1)} %bitcast.31, f32[128,2048]{1,0:T(8,128)S(1)} %convert_element_type.38, f32[1024]{0:T(1024)S(1)} %mul.70, bf16[]{:T(256)} %constant.34.clone.1), kind=kCustom, calls=%fused_computation.8 | custom fusion | flops 4194304 | bytes 7344130 | tf_op jit(solution)/shard_map/scatter | solution.py:27
  21.2 11.1 %copy.30 = bf16[2,768,2048]{2,0,1:T(2,128)(2,1)S(1)} copy(bf16[2,768,2048]{2,1,0:T(8,128)(2,1)} %bitcast.29) | data formatting | bytes 12582912 | tf_op jit(solution)/shard_map/reshape | solution.py:29
  32.3 0.0 copy-start.5
  32.3 156.8 %all_to_all.10 = bf16[2,768,2048]{2,0,1:T(2,128)(2,1)S(1)} all-to-all(bf16[2,768,2048]{2,0,1:T(2,128)(2,1)S(1)} %copy.30), channel_id=1, replica_groups=mesh['expert'=64,'tp'=8] {'expert'}, dimensions={1} | all-to-all | bytes 12582912 | tf_op jit(solution)/shard_map/all_to_all | solution.py:30
  189.1 0.0 copy-done.5
  189.1 3.9 fusion.8
  193.0 0.0 copy-done
  193.1 0.0 copy-done.2
  193.1 0.0 copy-start.3
  193.1 1.9 fusion.24
  195.0 1.9 add_convert_fusion
  196.9 18.8 %copy.32 = bf16[2,768,2048]{2,0,1:T(2,128)(2,1)} copy(bf16[2,768,2048]{2,1,0:T(8,128)(2,1)S(1)} %add_convert_fusion) | data formatting | bytes 12582912 | tf_op jit(solution)/shard_map/convert_element_type | solution.py:45
  215.6 19.8 %all-to-all-start.1 = ((bf16[2,768,2048]{2,0,1:T(2,128)(2,1)}), bf16[2,768,2048]{2,0,1:T(2,128)(2,1)}, u32[]{:S(2)}, u32[]{:S(2)}) async-start(bf16[2,768,2048]{2,0,1:T(2,128)(2,1)} %copy.32), calls=%async_computation.1 | async-start | bytes 12582912 | tf_op jit(solution)/shard_map/all_to_all | solution.py:46
  235.5 0.3 reduce-scatter.2.cloned.1.call-start
  235.8 164.4 %all-to-all-done.1 = bf16[2,768,2048]{2,0,1:T(2,128)(2,1)} async-done(((bf16[2,768,2048]{2,0,1:T(2,128)(2,1)}), bf16[2,768,2048]{2,0,1:T(2,128)(2,1)}, u32[]{:S(2)}, u32[]{:S(2)}) %all-to-all-start.1) | async-done | bytes 6291488 | tf_op jit(solution)/shard_map/all_to_all | solution.py:46
  400.1 8.3 %copy.33 = bf16[2,768,2048]{2,1,0:T(8,128)(2,1)} copy(bf16[2,768,2048]{2,0,1:T(2,128)(2,1)} %all-to-all-done.1) | data formatting | bytes 12582912 | tf_op jit(solution)/shard_map/all_to_all | solution.py:46
  408.5 12.5 %gather_fusion = bf16[1024,2048]{1,0:T(8,128)(2,1)} fusion(bf16[1536,2048]{1,0:T(8,128)(2,1)} %bitcast.28, s32[1024]{0:T(1024)S(1)} %broadcast_clamp_fusion), kind=kCustom, calls=%fused_computation | custom fusion | bytes 8392704 | tf_op jit(solution)/shard_map/gather | solution.py:47
  421.0 6.0 %convert_reduce_fusion = f32[128,2048]{1,0:T(8,128)} fusion(bf16[1024,2048]{1,0:T(8,128)(2,1)} %gather_fusion), kind=kLoop, calls=%fused_computation.3 | loop fusion | flops 3932160 | bytes 5242880 | tf_op jit(solution)/shard_map/reduce_sum | solution.py:48
  427.0 0.0 reduce-scatter.2.cloned.1.call-update
  427.0 78.6 %reduce-scatter.2.cloned.1.call-done = f32[16,2048]{1,0:T(8,128)} async-done(((f32[128,2048]{1,0:T(8,128)}), f32[16,2048]{1,0:T(8,128)}) %reduce-scatter.2.cloned.1.call-update) | async-done | bytes 131088 | tf_op jit(solution)/shard_map/reduce_scatter | solution.py:49
  (12 shorter events, 0.1 us)
Async XLA Ops:
  6.5 186.5 %copy-start = (bf16[2,96,2048]{2,1,0:T(8,128)(2,1)S(1)}, bf16[2,96,2048]{2,1,0:T(8,128)(2,1)}, u32[]{:S(2)}) copy-start(bf16[2,96,2048]{2,1,0:T(8,128)(2,1)} %param.13) | copy-start | bytes 2359300
  32.3 156.8 %copy-start.5 = (bf16[2,96,2048]{2,1,0:T(8,128)(2,1)S(1)}, bf16[2,96,2048]{2,1,0:T(8,128)(2,1)}, u32[]{:S(2)}) copy-start(bf16[2,96,2048]{2,1,0:T(8,128)(2,1)} %param.15) | copy-start | bytes 2359300
  189.1 4.0 copy-start.2
  189.1 4.0 copy-start.4
  193.1 1.9 copy-start.3
  215.6 184.5 %all-to-all-start.1 = ((bf16[2,768,2048]{2,0,1:T(2,128)(2,1)}), bf16[2,768,2048]{2,0,1:T(2,128)(2,1)}, u32[]{:S(2)}, u32[]{:S(2)}) async-start(bf16[2,768,2048]{2,0,1:T(2,128)(2,1)} %copy.32), calls=%async_computation.1 | async-start | bytes 12582912 | tf_op jit(solution)/shard_map/all_to_all | solution.py:46
  235.5 270.1 %reduce-scatter.2.cloned.1.call-start = ((), (), s32[]{:S(2)}) async-start(), calls=%async_computation.3 | async-start | bytes 1179648 | tf_op jit(solution)/shard_map/reduce_scatter | solution.py:49
  408.5 97.1 %copy-start.1 = (bf16[2,96,2048]{2,1,0:T(8,128)(2,1)S(1)}, bf16[2,96,2048]{2,1,0:T(8,128)(2,1)}, u32[]{:S(2)}) copy-start(bf16[2,96,2048]{2,1,0:T(8,128)(2,1)} %param.13) | copy-start | bytes 2359300
Sparse Core Ops, SparseCore 0:
  427.1 78.4 reduce-scatter.1
where the time goes:
time: 514 us; the launch traced here: 512 us
  waiting for transfers between devices  243 us (47%)
  blocking collectives  157 us (31%)
  local copies, waits for them, and re-layouts  52.9 us (10%)
  starting transfers between devices  20.1 us (4%)
  other arithmetic  18.4 us (4%)
  between operations  13.5 us (3%)
  matrix products  7.68 us (1%)
    all_to_all x1, waiting for transfers between devices, body(): lax.all_to_all(partial_value, 'expert', split_axis=1, concat_axis=1, tile...  164 us
    all_to_all x1, blocking collectives, body(): lax.all_to_all(outgoing, 'expert', split_axis=1, concat_axis=1, tiled=True)  157 us
    reduce_scatter x1, waiting for transfers between devices, body(): return lax.psum_scatter(combined, 'tp', scatter_dimension=0, tiled=True)  78.6 us
    all_to_all x1, starting transfers between devices, body(): lax.all_to_all(partial_value, 'expert', split_axis=1, concat_axis=1, tile...  19.8 us
    convert_element_type x1, local copies, waits for them, and re-layouts, body(): partial_value = partial_value.astype(jnp.bfloat16)  18.8 us
    gather x1, local copies, waits for them, and re-layouts, body(): returned.reshape(local_count * slot_count, feature_dim)[target]  12.5 us
    reshape x1, local copies, waits for them, and re-layouts, body(): outgoing = outgoing.reshape(local_count, slot_count, feature_dim)  11.1 us
    scatter x1, other arithmetic, body(): jnp.zeros((local_count * slot_count, feature_dim), jnp.bfloat16).at[target]  10.6 us
  transfers between devices with their start and end apart: 2, of which 2 were waited for; matrix products, arithmetic and copies ran while one was open for 0% of the time, Pallas kernels for 0%

commit v1 on v0

v1 whole, which is shorter than its diff:
```python
import jax
import jax.numpy as jnp
from jax import lax
from jax.experimental import pallas as pl
from jax.experimental.pallas import tpu as pltpu
from jax.sharding import PartitionSpec as P

TP = 8
OWNERS = 64
CAP = 12
LOCAL = 2
ROWS = LOCAL * CAP
F32 = jnp.float32
BF16 = jnp.bfloat16


def div12(x):
    return lax.shift_right_logical(x * 5462, 16)


def div24(x):
    return lax.shift_right_logical(x * 2731, 16)


def route_kernel(cot_ref, gates_ref, ids_ref, out_ref, select_ref):
    tokens, top = ids_ref.shape
    experts = OWNERS * LOCAL
    slots = experts * CAP
    lane = lax.broadcasted_iota(jnp.int32, (tokens, experts), 1)
    named = jnp.zeros((tokens, experts), F32)
    weight = jnp.zeros((tokens, experts), F32)
    for k in range(top):
        hit = ids_ref[:, k : k + 1] == lane
        named = jnp.where(hit, 1.0, named)
        weight = jnp.where(hit, gates_ref[:, k : k + 1], weight)
    row = lax.broadcasted_iota(jnp.int32, (tokens, tokens), 0)
    col = lax.broadcasted_iota(jnp.int32, (tokens, tokens), 1)
    lower = jnp.where(col < row, 1.0, 0.0).astype(BF16)
    before = jnp.dot(lower, named.astype(BF16), preferred_element_type=F32)
    place = jnp.where(named > 0.5, before, 64.0).astype(BF16)
    slot = lax.broadcasted_iota(jnp.int32, (slots, experts), 0)
    owner = div12(slot)
    spread = jnp.where(owner == lax.broadcasted_iota(jnp.int32, (slots, experts), 1), 1.0, 0.0)
    nt = (((1,), (1,)), ((), ()))
    place_of = lax.dot_general(spread.astype(BF16), place, nt, preferred_element_type=F32)
    weight_of = lax.dot_general(
        spread, weight, nt, preferred_element_type=F32, precision=lax.Precision.HIGHEST
    )
    want = (slot - owner * CAP).astype(F32)[:, :tokens]
    select = jnp.where(place_of == want, 1.0, 0.0)
    gate = jnp.sum(select * weight_of, axis=1, keepdims=True)
    select = select.astype(BF16)
    select_ref[...] = select
    picked = jnp.dot(select, cot_ref[...], preferred_element_type=F32)
    out_ref[...] = (picked * gate).astype(BF16)


def route(cot, gates, ids):
    tokens = cot.shape[0]
    slots = OWNERS * ROWS
    return pl.pallas_call(
        route_kernel,
        out_shape=(
            jax.ShapeDtypeStruct((slots, cot.shape[1]), BF16),
            jax.ShapeDtypeStruct((slots, tokens), BF16),
        ),
        name="route",
    )(cot, gates, ids)


def expert_kernel(x_ref, sg_ref, su_ref, wg_ref, wu_ref, wd_ref, out_ref):
    parts, block, width = x_ref.shape
    shard = sg_ref.shape[1]
    cols = sg_ref.shape[2]
    nt = (((1,), (1,)), ((), ()))
    tn = (((0,), (0,)), ((), ()))
    hidden = jnp.zeros((LOCAL * shard, block), F32)
    for k in range(parts):
        hidden += lax.dot_general(
            wd_ref[:, k * width : (k + 1) * width], x_ref[k], nt, preferred_element_type=F32
        )
    slot = lax.broadcasted_iota(jnp.int32, (1, block), 1)
    group = div24(slot)
    inner = slot - group * ROWS
    source = lax.broadcasted_iota(jnp.int32, (cols, block), 0)
    gate_rows = []
    up_rows = []
    for e in range(LOCAL):
        place = inner - e * CAP
        wanted = jnp.where((place >= 0) & (place < CAP), group * CAP + place, -1)
        move = jnp.where(source == wanted, 1.0, 0.0).astype(BF16)
        a = jnp.dot(sg_ref[e], move, preferred_element_type=F32)
        u = jnp.dot(su_ref[e], move, preferred_element_type=F32)
        h = hidden[e * shard : (e + 1) * shard]
        s = jax.nn.sigmoid(a)
        up_rows.append((h * a * s).astype(BF16))
        gate_rows.append((h * u * s * (1.0 + a * (1.0 - s))).astype(BF16))
    up = jnp.concatenate(up_rows, axis=0)
    gate = jnp.concatenate(gate_rows, axis=0)
    for k in range(parts):
        w = slice(k * width, (k + 1) * width)
        total = lax.dot_general(gate, wg_ref[:, w], tn, preferred_element_type=F32)
        total += lax.dot_general(up, wu_ref[:, w], tn, preferred_element_type=F32)
        out_ref[k] = total.astype(BF16)


def experts(x, saved_gate, saved_up, w_gate, w_up, w_down):
    parts, slots, width = x.shape
    steps = 2
    block = slots // steps
    local, shard, cols = saved_gate.shape
    flat = (local * shard, parts * width)
    saved = pl.BlockSpec((local, shard, cols // steps), lambda i: (0, 0, i))
    weight = pl.BlockSpec(flat, lambda i: (0, 0))
    moved = pl.BlockSpec((parts, block, width), lambda i: (0, i, 0))
    return pl.pallas_call(
        expert_kernel,
        grid=(steps,),
        in_specs=[moved, saved, saved, weight, weight, weight],
        out_specs=moved,
        out_shape=jax.ShapeDtypeStruct(x.shape, BF16),
        name="experts",
    )(x, saved_gate, saved_up, w_gate.reshape(flat), w_up.reshape(flat), w_down.reshape(flat))


def body(cotangent, gates, expert_ids, saved_gate, saved_up, w_gate, w_up, w_down):
    tokens, features = cotangent.shape
    width = features // TP
    me = lax.axis_index("tp")
    mine = lax.dynamic_slice(cotangent, (0, me * width), (tokens, width))
    outgoing, select = route(mine, gates, expert_ids)
    outgoing = outgoing.reshape(OWNERS, ROWS, width)
    arrived = lax.all_to_all(outgoing, "expert", split_axis=0, concat_axis=0, tiled=True)
    whole = lax.all_gather(arrived.reshape(OWNERS * ROWS, width), "tp", axis=0)
    partial_value = experts(whole, saved_gate, saved_up, w_gate, w_up, w_down)
    summed = lax.psum_scatter(partial_value, "tp", scatter_dimension=0, tiled=False)
    summed = summed.reshape(OWNERS, ROWS, width)
    returned = lax.all_to_all(summed, "expert", split_axis=0, concat_axis=0, tiled=True)
    combined = lax.dot_general(
        select,
        returned.reshape(OWNERS * ROWS, width),
        (((0,), (0,)), ((), ())),
        preferred_element_type=F32,
    )
    return lax.all_to_all(combined, "tp", split_axis=0, concat_axis=1, tiled=True)


def solution(mesh):
    in_specs = (
        P("expert", None),
        P("expert", None),
        P("expert", None),
        P("expert", "tp", None),
        P("expert", "tp", None),
        P("expert", "tp", None),
        P("expert", "tp", None),
        P("expert", "tp", None),
    )
    out_specs = P(("expert", "tp"), None)
    return jax.shard_map(body, mesh=mesh, in_specs=in_specs, out_specs=out_specs, check_vma=False)
```

time: 514 us -> 210 us (0.41)
  waiting for transfers between devices: 243 us -> 112 us
  blocking collectives: 157 us -> 52 us
  local copies, waits for them, and re-layouts: 52.9 us -> 4.38 us
  other arithmetic: 18.4 us -> 0 us
  Pallas kernels: 0 us -> 14.4 us
  matrix products: 7.68 us -> 0.27 us
  starting transfers between devices: 20.1 us -> 13.1 us
    all_to_all x1, waiting for transfers between devices: 164 us -> 21 us  [body(): lax.all_to_all(summed, 'expert', split_axis=0, concat_axis=0, tiled=True)]
    all_to_all x1 -> x2, blocking collectives: 157 us -> 52 us  [the longest x1 39.1 us: body(): lax.all_to_all(outgoing, 'expert', split_axis=0, concat_axis=0, tiled=True)]
    all_gather x0 -> x1, waiting for transfers between devices: none -> 43.8 us  [body(): whole = lax.all_gather(arrived.reshape(OWNERS * ROWS, width), 'tp', axis=0)]
    reduce_scatter x1, waiting for transfers between devices: 78.6 us -> 47.1 us  [body(): lax.psum_scatter(partial_value, 'tp', scatter_dimension=0, tiled=False)]
    convert_element_type x1 -> x0, local copies, waits for them, and re-layouts: 18.8 us -> none  [body(): partial_value = partial_value.astype(jnp.bfloat16)]
    pallas_call x0 -> x2, Pallas kernels: none -> 14.4 us  [the longest x1 10.9 us: experts(): pl.pallas_call(expert_kernel, grid=(steps,), in_specs=[moved, saved, save...]
    gather x1 -> x0, local copies, waits for them, and re-layouts: 12.5 us -> none  [body(): returned.reshape(local_count * slot_count, feature_dim)[target]]
    reshape x2 -> x0, local copies, waits for them, and re-layouts: 11.2 us -> none  [the longest x1 11.1 us: body(): outgoing = outgoing.reshape(local_count, slot_count, feature_dim)]
  transfers between devices with their start and end apart: 2 -> 3, of which waited for: 2 -> 3; matrix products, arithmetic and copies ran while one was open for 0% -> 0% of each run, Pallas kernels for 0% -> 0%
where the time goes in v1:
time: 210 us; the launch traced here: 209 us
  waiting for transfers between devices  112 us (53%)
  blocking collectives  52 us (25%)
  Pallas kernels  14.4 us (7%)
  between operations  13.4 us (6%)
  starting transfers between devices  13.1 us (6%)
  local copies, waits for them, and re-layouts  4.38 us (2%)
    reduce_scatter x1, waiting for transfers between devices, body(): lax.psum_scatter(partial_value, 'tp', scatter_dimension=0, tiled=False)  47.1 us
    all_gather x1, waiting for transfers between devices, body(): whole = lax.all_gather(arrived.reshape(OWNERS * ROWS, width), 'tp', axis=0)  43.8 us
    all_to_all x1, blocking collectives, body(): lax.all_to_all(outgoing, 'expert', split_axis=0, concat_axis=0, tiled=True)  39.1 us
    all_to_all x1, waiting for transfers between devices, body(): lax.all_to_all(summed, 'expert', split_axis=0, concat_axis=0, tiled=True)  21 us
    all_to_all x1, starting transfers between devices, body(): lax.all_to_all(summed, 'expert', split_axis=0, concat_axis=0, tiled=True)  13 us
    all_to_all x1, blocking collectives, body(): lax.all_to_all(combined, 'tp', split_axis=0, concat_axis=1, tiled=True)  12.9 us
    pallas_call x1, Pallas kernels, experts(): pl.pallas_call(expert_kernel, grid=(steps,), in_specs=[moved, saved, save...  10.9 us
  transfers between devices with their start and end apart: 3, of which 3 were waited for; matrix products, arithmetic and copies ran while one was open for 0% of the time, Pallas kernels for 0%

profile of v1, /device:TPU:1, one launch (start us, length us, event | category | flops | bytes accessed | tf_op | source)
XLA Modules:
  0.0 209.5 jit_solution(7183843569470625610)
XLA Ops:
  6.5 0.0 copy-start
  6.5 0.0 all-gather.2.cloned.1.call-start
  6.5 1.5 copy.16.gates_ref
  8.0 1.4 copy.17.ids_ref
  9.4 0.0 copy-done
  9.4 0.6 constant_dynamic-slice_fusion.cot_ref
  10.1 3.5 %route.1 = (bf16[1536,256]{1,0:T(8,128)(2,1)}, bf16[1536,128]{1,0:T(8,128)(2,1)}) custom-call(bf16[128,256]{1,0:T(8,128)(2,1)} %constant_dynamic-slice_fusion.cot_ref, f32[128,8]{1,0:T(8,128)} %copy.16.gates_ref, s32[128,8]{1,0:T(8,128)} %copy.17.ids_ref), custom_call_target="tpu_custom_call" | custom-call | tf_op jit(solution)/shard_map/route/pallas_call | solution.py:61
  13.6 39.1 %all_to_all.26 = bf16[64,24,256]{2,1,0:T(8,128)(2,1)} all-to-all(bf16[64,24,256]{2,1,0:T(8,128)(2,1)} %bitcast.20), channel_id=1, replica_groups=mesh['expert'=64,'tp'=8] {'expert'}, dimensions={0} | all-to-all | bytes 1572864 | tf_op jit(solution)/shard_map/all_to_all | solution.py:133
  52.7 0.0 all-gather.2.cloned.1.call-update
  52.7 0.0 reduce-scatter.2.cloned.1.call-start
  52.8 43.8 %all-gather.2.cloned.1.call-done.x_ref = bf16[8,1536,256]{2,1,0:T(8,128)(2,1)} async-done(((bf16[1,1536,256]{2,1,0:T(8,128)(2,1)}), bf16[8,1536,256]{2,1,0:T(8,128)(2,1)}) %all-gather.2.cloned.1.call-update) | async-done | bytes 6291472 | tf_op jit(solution)/shard_map/all_gather | solution.py:134
  96.6 10.9 %experts.1 = bf16[8,1536,256]{2,1,0:T(8,128)(2,1)} custom-call(bf16[8,1536,256]{2,1,0:T(8,128)(2,1)} %all-gather.2.cloned.1.call-done.x_ref, bf16[2,96,768]{2,1,0:T(8,128)(2,1)} %sg_ref.1, bf16[2,96,768]{2,1,0:T(8,128)(2,1)} %su_ref.1, bf16[192,2048]{1,0:T(8,128)(2,1)} %bitcast.21, bf16[192,2048]{1,0:T(8,128)(2,1)} %bitcast.22, bf16[192,2048]{1,0:T(8,128)(2,1)} %bitcast.23), custom_call_target="tpu_custom_call" | custom-call | tf_op jit(solution)/shard_map/experts/pallas_call | solution.py:116
  107.5 0.0 copy-start.1
  107.5 0.0 reduce-scatter.2.cloned.1.call-update
  107.5 47.1 %reduce-scatter.2.cloned.1.call-done = bf16[1,1536,256]{2,1,0:T(8,128)(2,1)} async-done(((bf16[8,1536,256]{2,1,0:T(8,128)(2,1)}), bf16[1,1536,256]{2,1,0:T(8,128)(2,1)}) %reduce-scatter.2.cloned.1.call-update) | async-done | bytes 786448 | tf_op jit(solution)/shard_map/reduce_scatter | solution.py:136
  154.6 13.0 %all-to-all-start.1 = ((bf16[64,24,256]{2,1,0:T(8,128)(2,1)}), bf16[64,24,256]{2,1,0:T(8,128)(2,1)S(1)}, u32[]{:S(2)}, u32[]{:S(2)}) async-start(bf16[64,24,256]{2,1,0:T(8,128)(2,1)} %bitcast.19), calls=%async_computation.2 | async-start | bytes 1572864 | tf_op jit(solution)/shard_map/all_to_all | solution.py:138
  167.6 0.0 copy-done.1
  167.6 0.2 copy.18
  167.8 21.0 %all-to-all-done.1 = bf16[64,24,256]{2,1,0:T(8,128)(2,1)S(1)} async-done(((bf16[64,24,256]{2,1,0:T(8,128)(2,1)}), bf16[64,24,256]{2,1,0:T(8,128)(2,1)S(1)}, u32[]{:S(2)}, u32[]{:S(2)}) %all-to-all-start.1) | async-done | bytes 786464 | tf_op jit(solution)/shard_map/all_to_all | solution.py:138
  188.8 0.3 fusion
  189.1 12.9 %all_to_all.27 = f32[8,16,256]{2,1,0:T(8,128)S(1)} all-to-all(f32[8,16,256]{2,1,0:T(8,128)S(1)} %fusion), channel_id=1, replica_groups=mesh['expert'=64,'tp'=8] {'tp'}, dimensions={0} | all-to-all | bytes 262144 | tf_op jit(solution)/shard_map/all_to_all | solution.py:145
  202.0 0.7 copy.20
Async XLA Ops:
  6.5 2.9 %copy-start = (bf16[128,2048]{1,0:T(8,128)(2,1)S(1)}, bf16[128,2048]{1,0:T(8,128)(2,1)}, u32[]{:S(2)}) copy-start(bf16[128,2048]{1,0:T(8,128)(2,1)} %param.8) | copy-start | bytes 1572868
  6.5 90.0 %all-gather.2.cloned.1.call-start = ((), (), s32[]{:S(2)}) async-start(), calls=%async_computation.4 | async-start | bytes 7077888 | tf_op jit(solution)/shard_map/all_gather | solution.py:134
  52.7 101.9 %reduce-scatter.2.cloned.1.call-start = ((), (), s32[]{:S(2)}) async-start(), calls=%async_computation.5 | async-start | bytes 7077888 | tf_op jit(solution)/shard_map/reduce_scatter | solution.py:136
  107.5 60.2 %copy-start.1 = (bf16[1536,128]{1,0:T(8,128)(2,1)S(1)}, bf16[1536,128]{1,0:T(8,128)(2,1)}, u32[]{:S(2)}) copy-start(bf16[1536,128]{1,0:T(8,128)(2,1)} %get-tuple-element.7) | copy-start | bytes 1179652
  154.6 34.2 %all-to-all-start.1 = ((bf16[64,24,256]{2,1,0:T(8,128)(2,1)}), bf16[64,24,256]{2,1,0:T(8,128)(2,1)S(1)}, u32[]{:S(2)}, u32[]{:S(2)}) async-start(bf16[64,24,256]{2,1,0:T(8,128)(2,1)} %bitcast.19), calls=%async_computation.2 | async-start | bytes 1572864 | tf_op jit(solution)/shard_map/all_to_all | solution.py:138
Sparse Core Ops, SparseCore 0:
  52.9 43.6 all-gather.1
  107.6 46.9 reduce-scatter.1
